TPU v7x, 32 devices: a whole 2x2x4 slice. The times are simulated.
32 devices in a mesh: dp: 8 (over z, y), tensor: 4 (over x, core).
Axes of the slice: x: 2, y: 2, z: 4, core: 2. Of those that a mesh axis runs over, the one named last changes fastest.
Arguments:
- gate_pre: bfloat16 [512, 16384], P('dp', 'tensor'), may hold values from -6 to 6
- up_pre: bfloat16 [512, 16384], P('dp', 'tensor'), may hold values from -6 to 6
- cotangent: bfloat16 [512, 4096], P(('dp', 'tensor')), may hold values from -6 to 6
- down_blocks: bfloat16 [4, 256, 4096], P('tensor'), may hold values from -0.1875 to 0.1875
- live_blocks: int32 [4, 256], P('tensor'), may hold values from 0 to 4095, as said below
Outputs:
- layer_out: bfloat16 [512, 4096], P(('dp', 'tensor'))
- gate_grad: bfloat16 [512, 16384], P('dp', 'tensor')
- up_grad: bfloat16 [512, 16384], P('dp', 'tensor')
- weight_grad: float32 [4, 256, 4096], P('tensor', 'dp')
Inputs may be any that keep to these rules, and one draw needn't show every extreme that they name: `live_blocks`: in each row, the 256 numbers are distinct; block 0 and the last block number are live in every shard.
All inputs are finite; a program needn't handle non-finite values.
Results may differ from a plain program's by a relative error of at most 0.013.
Values may be sent and summed in bfloat16 or wider, within the bound.
A program may use at most 64 MiB of HBM per device.

v0:
```python
import math

import jax
import jax.numpy as jnp
from jax import lax
from jax.sharding import PartitionSpec as P

D = 4096
BLOCK = 64


def on_device(gate_pre, up_pre, cotangent, down_blocks, live_blocks):
    rows, ff_dev = gate_pre.shape
    live = live_blocks.shape[1]
    hid_count = ff_dev // BLOCK
    col_count = D // BLOCK
    block_ids = live_blocks[0]
    hid_ids = block_ids // col_count
    col_ids = block_ids % col_count
    weights = down_blocks[0].reshape(live, BLOCK, BLOCK)
    col_onehot = (col_ids[:, None] == jnp.arange(col_count)[None, :]).astype(jnp.float32)
    hid_onehot = (hid_ids[:, None] == jnp.arange(hid_count)[None, :]).astype(jnp.float32)
    gate32 = gate_pre.astype(jnp.float32)
    up32 = up_pre.astype(jnp.float32)
    sig = jax.nn.sigmoid(gate32)
    silu_g = gate32 * sig
    hidden = (silu_g * up32).astype(jnp.bfloat16)
    hsel = hidden.T.reshape(hid_count, BLOCK, rows)[hid_ids]
    prod = jnp.einsum("lkt,lkj->ljt", hsel, weights, preferred_element_type=jnp.float32)
    spread = jnp.einsum("ljt,lc->cjt", prod, col_onehot).reshape(D, rows).T
    layer_out = lax.psum_scatter(
        spread.astype(jnp.bfloat16), "tensor", scatter_dimension=0, tiled=True
    )
    cot_full = lax.all_gather(cotangent, "tensor", axis=0, tiled=True)
    dysel = cot_full.T.reshape(col_count, BLOCK, rows)[col_ids]
    dh_blk = jnp.einsum("ljt,lkj->lkt", dysel, weights, preferred_element_type=jnp.float32)
    hidden_grad = jnp.einsum("lkt,lh->hkt", dh_blk, hid_onehot).reshape(ff_dev, rows).T
    gate_grad = (hidden_grad * up32 * sig * (1.0 + gate32 * (1.0 - sig))).astype(jnp.bfloat16)
    up_grad = (hidden_grad * silu_g).astype(jnp.bfloat16)
    scale = 1.0 / math.sqrt(rows * lax.axis_size("dp"))
    term = jnp.einsum("lkt,ljt->lkj", hsel, dysel, preferred_element_type=jnp.float32)
    term = term.reshape(live, BLOCK * BLOCK) * scale
    weight_grad = lax.psum_scatter(term, "dp", scatter_dimension=0, tiled=True)
    return (layer_out, gate_grad, up_grad, weight_grad[None])


def solution(mesh):
    in_specs = (
        P("dp", "tensor"),
        P("dp", "tensor"),
        P(("dp", "tensor"), None),
        P("tensor", None, None),
        P("tensor", None),
    )
    out_specs = (
        P(("dp", "tensor"), None),
        P("dp", "tensor"),
        P("dp", "tensor"),
        P("tensor", "dp", None),
    )
    return jax.shard_map(
        on_device, mesh=mesh, in_specs=in_specs, out_specs=out_specs, check_vma=False
    )
```

profile of v0, /device:TPU:0, one launch (start us, length us, event | category | flops | bytes accessed | tf_op | source)
XLA Modules:
  0.0 188.4 jit_solution(2527760053779191711)
XLA Ops:
  7.2 8.9 %all_gather.3 = bf16[64,4096]{1,0:T(8,128)(2,1)S(1)} all-gather(bf16[16,4096]{1,0:T(8,128)(2,1)} %param.7), channel_id=1, replica_groups=mesh['dp'=8,'tensor'=4] {'tensor'}, dimensions={0}, use_global_device_ids=true | all-gather | bytes 655360 | tf_op jit(solution)/shard_map/all_gather | solution.py:34
  16.1 0.5 copy.22
  16.6 0.7 compare_select_fusion
  17.3 3.3 %copy.17 = bf16[1,256,4096]{1,2,0:T(8,128)(2,1)S(1)} copy(bf16[1,256,4096]{2,1,0:T(8,128)(2,1)} %param.8) | data formatting | bytes 4194304 | tf_op args[3]
  20.6 6.6 %copy.19 = bf16[256,64,64]{2,1,0:T(8,128)(2,1)} copy(bf16[256,64,64]{0,2,1:T(8,128)(2,1)S(1)} %bitcast.57) | data formatting | bytes 4194304 | tf_op jit(solution)/shard_map/reshape;squeeze | solution.py:20
  27.2 3.0 %gather_fusion.1 = bf16[256,64,64]{2,1,0:T(8,128)(2,1)} fusion(bf16[64,64,64]{2,1,0:T(8,128)(2,1)S(1)} %bitcast.53, s32[1024]{0:T(1024)S(1)} %pad_clamp_fusion), kind=kCustom, calls=%fused_computation.1 | custom fusion | bytes 4195328 | tf_op jit(solution)/shard_map/gather | solution.py:35
  30.2 5.8 %convolution_bitcast_fusion = bf16[256,64,64]{1,2,0:T(8,128)(2,1)S(1)} fusion(bf16[256,64,64]{2,1,0:T(8,128)(2,1)} %gather_fusion.1, bf16[256,64,64]{2,1,0:T(8,128)(2,1)} %copy.19), kind=kOutput, calls=%fused_computation.5 | convolution fusion | flops 134217728 | bytes 6291456 | tf_op jit(solution)/shard_map/ljt,lkj->lkt/dot_general | solution.py:36
  36.0 2.5 %fusion = f32[64,64,64]{1,0,2:T(8,128)S(1)} fusion(bf16[256,64,64]{1,2,0:T(8,128)(2,1)S(1)} %convolution_bitcast_fusion, s32[256]{0:T(256)S(1)} %get-tuple-element.17), kind=kOutput, calls=%fused_computation.2 | convolution fusion | flops 134234112 | bytes 3146752 | tf_op jit(solution)/shard_map/lkt,lh->hkt/dot_general | solution.py:37
  38.6 0.7 reshape.160
  39.2 2.8 %fusion.10 = (bf16[64,4096]{1,0:T(8,128)(2,1)}, bf16[64,4096]{1,0:T(8,128)(2,1)}, bf16[4096,64]{0,1:T(8,128)(2,1)S(1)}) fusion(f32[4096,64]{0,1:T(8,128)S(1)} %reshape.160, bf16[64,4096]{1,0:T(8,128)(2,1)} %param.5, bf16[64,4096]{1,0:T(8,128)(2,1)} %param.6), kind=kLoop, calls=%fused_computation.22 | loop fusion | flops 4456448 | bytes 3670016 | tf_op jit(solution)/shard_map/convert_element_type | solution.py:39
  42.0 0.5 copy.16
  42.5 3.0 %gather_fusion = bf16[256,64,64]{2,1,0:T(8,128)(2,1)} fusion(bf16[64,64,64]{2,1,0:T(8,128)(2,1)S(1)} %bitcast.54, s32[1024]{0:T(1024)S(1)} %pad_clamp_fusion.1), kind=kCustom, calls=%fused_computation | custom fusion | bytes 4195328 | tf_op jit(solution)/shard_map/gather | solution.py:28
  45.5 9.0 %broadcast_multiply_fusion = f32[256,64,64]{2,1,0:T(8,128)} fusion(bf16[256,64,64]{2,1,0:T(8,128)(2,1)} %gather_fusion, bf16[256,64,64]{2,1,0:T(8,128)(2,1)} %gather_fusion.1), kind=kOutput, calls=%fused_computation.4 | convolution fusion | flops 135266304 | bytes 8388608 | tf_op jit(solution)/shard_map/lkt,ljt->lkj/dot_general | solution.py:41
  54.5 7.7 %copy.27 = f32[256,64,64]{0,2,1:T(8,128)} copy(f32[256,64,64]{2,1,0:T(8,128)} %broadcast_multiply_fusion) | data formatting | bytes 8388608 | tf_op jit(solution)/shard_map/mul | solution.py:42
  62.3 5.6 %copy.34 = f32[256,4096]{1,0:T(8,128)} copy(f32[256,4096]{0,1:T(8,128)} %bitcast.55) | data formatting | bytes 8388608
  68.0 7.0 %convolution_bitcast_fusion.1 = bf16[256,64,64]{1,2,0:T(8,128)(2,1)} fusion(bf16[256,64,64]{2,1,0:T(8,128)(2,1)} %gather_fusion, bf16[256,64,64]{2,1,0:T(8,128)(2,1)} %copy.19), kind=kOutput, calls=%fused_computation.6 | convolution fusion | flops 134217728 | bytes 6291456 | tf_op jit(solution)/shard_map/lkt,lkj->ljt/dot_general | solution.py:29
  74.9 7.1 %copy.20 = bf16[256,64,64]{0,2,1:T(8,128)(2,1)S(1)} copy(bf16[256,64,64]{1,2,0:T(8,128)(2,1)} %convolution_bitcast_fusion.1) | data formatting | bytes 4194304 | tf_op jit(solution)/shard_map/lkt,lkj->ljt/dot_general | solution.py:29
  82.0 1.1 convolution_convert_fusion
  83.2 2.2 %copy.21 = bf16[64,64,64]{1,0,2:T(8,128)(2,1)S(1)} copy(bf16[64,64,64]{2,0,1:T(8,128)(2,1)S(1)} %convolution_convert_fusion) | data formatting | bytes 1048576 | tf_op jit(solution)/shard_map/convert_element_type | solution.py:32
  85.4 1.6 convert_element_type.30
  87.1 70.2 %reduce-scatter.7.cloned.1.call-done = f32[32,4096]{1,0:T(8,128)} async-done(((f32[256,4096]{1,0:T(8,128)}), f32[32,4096]{1,0:T(8,128)}) %reduce-scatter.7.cloned.1.call-update) | async-done | bytes 524304
  157.2 1.6 copy.35
  158.9 1.4 copy.28
  160.2 21.4 %reduce-scatter.5.cloned.1.call-done = bf16[16,4096]{1,0:T(8,128)(2,1)} async-done(((bf16[64,4096]{1,0:T(8,128)(2,1)}), bf16[16,4096]{1,0:T(8,128)(2,1)}) %reduce-scatter.5.cloned.1.call-update) | async-done | bytes 131088 | tf_op jit(solution)/shard_map/reduce_scatter | solution.py:31
  (10 shorter events, 0.2 us)
Async XLA Ops:
  7.2 150.1 %reduce-scatter.7.cloned.1.call-start = ((), (), s32[]{:S(2)}) async-start(), calls=%async_computation.3 | async-start | bytes 4718592
  20.5 6.6 %copy-start = (s32[1,256]{1,0:T(1,128)S(1)}, s32[1,256]{1,0:T(1,128)}, u32[]{:S(2)}) copy-start(s32[1,256]{1,0:T(1,128)} %param.9) | copy-start | bytes 3076
  67.9 113.7 %reduce-scatter.5.cloned.1.call-start = ((), (), s32[]{:S(2)}) async-start(), calls=%async_computation.2 | async-start | bytes 655360 | tf_op jit(solution)/shard_map/reduce_scatter | solution.py:31
Sparse Core Ops, SparseCore 0:
  68.0 89.1 reduce-scatter.6
  160.3 21.2 reduce-scatter.4
where the time goes:
time: 189 us; the launch traced here: 188 us
  waiting for transfers between devices  91.6 us (48%)
  local copies, waits for them, and re-layouts  44.9 us (24%)
  matrix products  25.4 us (13%)
  between operations  14.1 us (7%)
  blocking collectives  8.86 us (5%)
  other arithmetic  3.5 us (2%)
    unnamed x3, waiting for transfers between devices  70.2 us
    reduce_scatter x1, waiting for transfers between devices, on_device(): lax.psum_scatter(spread.astype(jnp.bfloat16), 'tensor', scatter_dimension...  21.4 us
    unnamed x6, local copies, waits for them, and re-layouts  11.9 us
    dot_general x1, matrix products, on_device(): jnp.einsum('lkt,ljt->lkj', hsel, dysel, preferred_element_type=jnp.float32)  8.98 us
    all_gather x1, blocking collectives, on_device(): cot_full = lax.all_gather(cotangent, 'tensor', axis=0, tiled=True)  8.86 us
    mul x1, local copies, waits for them, and re-layouts, on_device(): term = term.reshape(live, BLOCK * BLOCK) * scale  7.75 us
    dot_general x1, local copies, waits for them, and re-layouts, on_device(): jnp.einsum('lkt,lkj->ljt', hsel, weights, preferred_element_type=jnp.floa...  7.1 us
    dot_general x1, matrix products, on_device(): jnp.einsum('lkt,lkj->ljt', hsel, weights, preferred_element_type=jnp.floa...  6.96 us
  transfers between devices with their start and end apart: 2, of which 2 were waited for; matrix products, arithmetic and copies ran while one was open for 12% of the time, Pallas kernels for 0%

commit v1 on v0

--- a/solution.py
+++ b/solution.py
@@ -1,15 +1,20 @@
+import functools
 import math
 
 import jax
 import jax.numpy as jnp
 from jax import lax
+from jax.experimental import pallas as pl
+from jax.experimental.pallas import tpu as pltpu
 from jax.sharding import PartitionSpec as P
 
 D = 4096
 BLOCK = 64
-
-
-def on_device(gate_pre, up_pre, cotangent, down_blocks, live_blocks):
+COLS = D // BLOCK
+LANES = 2 * BLOCK
+
+
+def plain(gate_pre, up_pre, cotangent, down_blocks, live_blocks):
     rows, ff_dev = gate_pre.shape
     live = live_blocks.shape[1]
     hid_count = ff_dev // BLOCK
@@ -44,6 +49,138 @@
     return (layer_out, gate_grad, up_grad, weight_grad[None])
 
 
+def pair_at(ids_ref, p, half):
+    a = (p // half) * (2 * half) + p % half
+    first, second = ids_ref[0, a], ids_ref[0, a + half]
+    return first // COLS, second // COLS, first % COLS, second % COLS
+
+
+def lane_low(shape):
+    return lax.broadcasted_iota(jnp.int32, shape, 1) < BLOCK
+
+
+def flip_in(x32, out_ref, c):
+    both = jnp.concatenate([x32, x32], axis=0).T.astype(jnp.bfloat16)
+    out_ref[2 * c] = both[:BLOCK]
+    out_ref[2 * c + 1] = both[BLOCK:]
+
+
+def flip_out(acc_ref, c):
+    both = jnp.concatenate([acc_ref[2 * c], acc_ref[2 * c + 1]], axis=0).T
+    return both[:BLOCK] + both[BLOCK:]
+
+
+def chunk_of(c):
+    return pl.ds(pl.multiple_of(c * LANES, LANES), LANES)
+
+
+def term_kernel(half, scale, ids_ref, gate_ref, up_ref, cot_ref, term_ref, ht_ref, ct_ref):
+    def turn(c, _):
+        at = chunk_of(c)
+        gate = gate_ref[:, at].astype(jnp.float32)
+        hidden = gate * jax.nn.sigmoid(gate) * up_ref[:, at].astype(jnp.float32)
+        flip_in(hidden.astype(jnp.bfloat16).astype(jnp.float32), ht_ref, c)
+        flip_in(cot_ref[:, at].astype(jnp.float32), ct_ref, c)
+        return 0
+
+    lax.fori_loop(0, gate_ref.shape[1] // LANES, turn, 0, unroll=4)
+    low = lane_low((BLOCK, LANES))
+
+    def pair(p, _):
+        ha, hb, ca, cb = pair_at(ids_ref, p, half)
+        h = jnp.concatenate([ht_ref[ha], ht_ref[hb]], axis=0)
+        c = jnp.concatenate([ct_ref[ca], ct_ref[cb]], axis=0)
+        r = lax.dot_general(h, c, (((1,), (1,)), ((), ())), preferred_element_type=jnp.float32)
+        term_ref[p] = (jnp.where(low, r[:BLOCK], r[BLOCK:]) * (0.5 * scale)).astype(jnp.bfloat16)
+        return 0
+
+    lax.fori_loop(0, term_ref.shape[0], pair, 0, unroll=8)
+
+
+def product_kernel(half, ids_ref, gate_ref, up_ref, ht_ref, ct_ref, w_ref, part_ref, gg_ref, ug_ref, out_acc, dh_acc):
+    out_acc[...] = jnp.zeros_like(out_acc)
+    dh_acc[...] = jnp.zeros_like(dh_acc)
+    low = lane_low((BLOCK, LANES))
+    keep_a = low.astype(jnp.float32).astype(jnp.bfloat16)
+    keep_b = (1.0 - low.astype(jnp.float32)).astype(jnp.bfloat16)
+    group = 4
+
+    def pairs(g, _):
+        done = []
+        for i in range(group):
+            p = g * group + i
+            ha, hb, ca, cb = pair_at(ids_ref, p, half)
+            w = w_ref[p]
+            h = ht_ref[ha] * keep_a + ht_ref[hb] * keep_b
+            r1 = lax.dot_general(w, h, (((0,), (0,)), ((), ())), preferred_element_type=jnp.float32)
+            c = jnp.concatenate([ct_ref[ca] * keep_a, ct_ref[cb] * keep_b], axis=0)
+            r2 = jnp.dot(w, c, preferred_element_type=jnp.float32)
+            done.append((ha, hb, ca, cb, r1, r2))
+        for ha, hb, ca, cb, r1, r2 in done:
+            out_acc[ca] += jnp.where(low, r1[:BLOCK], 0.0)
+            out_acc[cb] += jnp.where(low, 0.0, r1[BLOCK:])
+            dh_acc[ha] += jnp.where(low, r2, 0.0)
+            dh_acc[hb] += jnp.where(low, 0.0, r2)
+        return 0
+
+    lax.fori_loop(0, w_ref.shape[0] // group, pairs, 0)
+
+    def finish(c, _):
+        at = chunk_of(c)
+        part_ref[:, at] = flip_out(out_acc, c).astype(jnp.bfloat16)
+        dh = flip_out(dh_acc, c)
+        gate = gate_ref[:, at].astype(jnp.float32)
+        up = up_ref[:, at].astype(jnp.float32)
+        sig = jax.nn.sigmoid(gate)
+        gg_ref[:, at] = (dh * up * sig * (1.0 + gate * (1.0 - sig))).astype(jnp.bfloat16)
+        ug_ref[:, at] = (dh * (gate * sig)).astype(jnp.bfloat16)
+        return 0
+
+    lax.fori_loop(0, gate_ref.shape[1] // LANES, finish, 0, unroll=4)
+
+
+def vmem(n):
+    return [pl.BlockSpec(memory_space=pltpu.VMEM)] * n
+
+
+SMEM_SPEC = pl.BlockSpec(memory_space=pltpu.SMEM)
+
+
+def on_device(gate_pre, up_pre, cotangent, down_blocks, live_blocks):
+    rows, ff_dev = gate_pre.shape
+    live = live_blocks.shape[1]
+    n_dp, n_tensor = lax.axis_size("dp"), lax.axis_size("tensor")
+    if rows != BLOCK or ff_dev != D or live % (2 * n_dp) or live % 8:
+        return plain(gate_pre, up_pre, cotangent, down_blocks, live_blocks)
+    half = live // n_dp // 2
+    scale = 1.0 / math.sqrt(rows * n_dp)
+    cot_full = lax.all_gather(cotangent, "tensor", axis=0, tiled=True)
+    stack = jax.ShapeDtypeStruct((COLS, BLOCK, LANES), jnp.bfloat16)
+    term, ht, ct = pl.pallas_call(
+        functools.partial(term_kernel, half, scale),
+        out_shape=(jax.ShapeDtypeStruct((live // 2, BLOCK, LANES), jnp.bfloat16), stack, stack),
+        in_specs=[SMEM_SPEC] + vmem(3),
+        out_specs=tuple(vmem(3)),
+        cost_estimate=pl.CostEstimate(flops=10**9, bytes_accessed=2**23, transcendentals=2**18),
+    )(live_blocks, gate_pre, up_pre, cot_full)
+    summed = lax.psum_scatter(term, "dp", scatter_dimension=0, tiled=True)
+    paired = down_blocks[0].reshape(n_dp, 2, half, BLOCK, BLOCK).transpose(0, 2, 3, 1, 4)
+    paired = paired.reshape(live // 2, BLOCK, LANES)
+    whole = jax.ShapeDtypeStruct((rows, D), jnp.bfloat16)
+    part, gate_grad, up_grad = pl.pallas_call(
+        functools.partial(product_kernel, half),
+        out_shape=(whole, whole, whole),
+        in_specs=[SMEM_SPEC] + vmem(5),
+        out_specs=tuple(vmem(3)),
+        scratch_shapes=[pltpu.VMEM((COLS, BLOCK, LANES), jnp.float32)] * 2,
+        cost_estimate=pl.CostEstimate(flops=10**9, bytes_accessed=2**24, transcendentals=2**18),
+    )(live_blocks, gate_pre, up_pre, ht, ct, paired)
+    shares = lax.all_to_all(part.reshape(n_tensor, rows // n_tensor, D), "tensor", 0, 0)
+    layer_out = jnp.sum(shares.astype(jnp.float32), axis=0).astype(jnp.bfloat16)
+    grad = summed.astype(jnp.float32).reshape(half, BLOCK, 2, BLOCK).transpose(2, 0, 1, 3)
+    return (layer_out, gate_grad, up_grad, grad.reshape(1, 2 * half, BLOCK * BLOCK))
+
+
 def solution(mesh):
     in_specs = (
         P("dp", "tensor"),

time: 189 us -> 106 us (0.56)
  waiting for transfers between devices: 91.6 us -> 16.4 us
  matrix products: 25.4 us -> 0 us
  Pallas kernels: 0 us -> 23.1 us
  local copies, waits for them, and re-layouts: 44.9 us -> 28.8 us
  blocking collectives: 8.86 us -> 22.4 us
  other arithmetic: 3.5 us -> 0.74 us
    unnamed x3 -> x1, waiting for transfers between devices: 70.2 us -> 0.02 us
    dot_general x5 -> x0, matrix products: 25.4 us -> none  [the longest x1 8.98 us: on_device(): jnp.einsum('lkt,ljt->lkj', hsel, dysel, preferred_element_type=jnp.float32)]
    pallas_call x0 -> x2, Pallas kernels: none -> 23.1 us  [the longest x1 13.3 us: on_device(): pl.pallas_call(functools.partial(product_kernel, half), out_shape=(whole,...]
    all_to_all x0 -> x1, blocking collectives: none -> 12.3 us  [on_device(): lax.all_to_all(part.reshape(n_tensor, rows // n_tensor, D), 'tensor', 0, 0)]
    unnamed x6 -> x2, local copies, waits for them, and re-layouts: 11.9 us -> 0.01 us
    another operation x1 -> x2, local copies, waits for them, and re-layouts: 6.63 us -> 18.2 us  [on_device(): down_blocks[0].reshape(n_dp, 2, half, BLOCK, BLOCK).transpose(0, 2, 3, 1, 4)]
    reshape x1 -> x4, local copies, waits for them, and re-layouts: 0.65 us -> 10.6 us  [the longest x1 7.82 us: on_device(): paired = paired.reshape(live // 2, BLOCK, LANES)]
    mul x1 -> x0, local copies, waits for them, and re-layouts: 7.75 us -> none  [on_device(): term = term.reshape(live, BLOCK * BLOCK) * scale]
  transfers between devices with their start and end apart: 2 -> 1, of which waited for: 2 -> 1; matrix products, arithmetic and copies ran while one was open for 12% -> 25% of each run, Pallas kernels for 0% -> 13%
where the time goes in v1:
time: 106 us
  local copies, waits for them, and re-layouts  28.8 us (27%)
  Pallas kernels  23.1 us (22%)
  blocking collectives  22.4 us (21%)
  waiting for transfers between devices  16.4 us (15%)
  between operations  14.1 us (13%)
    another operation x2, local copies, waits for them, and re-layouts, on_device(): down_blocks[0].reshape(n_dp, 2, half, BLOCK, BLOCK).transpose(0, 2, 3, 1, 4)  18.2 us
    reduce_scatter x1, waiting for transfers between devices, on_device(): summed = lax.psum_scatter(term, 'dp', scatter_dimension=0, tiled=True)  16.4 us
    pallas_call x1, Pallas kernels, on_device(): pl.pallas_call(functools.partial(product_kernel, half), out_shape=(whole,...  13.3 us
    all_to_all x1, blocking collectives, on_device(): lax.all_to_all(part.reshape(n_tensor, rows // n_tensor, D), 'tensor', 0, 0)  12.3 us
    all_gather x1, blocking collectives, on_device(): cot_full = lax.all_gather(cotangent, 'tensor', axis=0, tiled=True)  10.2 us
    pallas_call x1, Pallas kernels, on_device(): pl.pallas_call(functools.partial(term_kernel, half, scale), out_shape=(ja...  9.78 us
    reshape x1, local copies, waits for them, and re-layouts, on_device(): paired = paired.reshape(live // 2, BLOCK, LANES)  7.82 us
    reshape x3, local copies, waits for them, and re-layouts, on_device(): grad.reshape(1, 2 * half, BLOCK * BLOCK)  2.82 us
  transfers between devices with their start and end apart: 1, of which 1 were waited for; matrix products, arithmetic and copies ran while one was open for 25% of the time, Pallas kernels for 13%

profile of v1, /device:TPU:0, one launch (start us, length us, event | category | flops | bytes accessed | tf_op | source)
XLA Modules:
  0.0 105.6 jit_solution(7640264200669721822)
XLA Ops:
  7.2 0.0 reduce-scatter.2.cloned.1.call-start
  7.2 10.2 %all_gather.3.cot_ref = bf16[64,4096]{1,0:T(8,128)(2,1)} all-gather(bf16[16,4096]{1,0:T(8,128)(2,1)} %param.7), channel_id=1, replica_groups=mesh['dp'=8,'tensor'=4] {'tensor'}, dimensions={0}, use_global_device_ids=true | all-gather | bytes 655360 | tf_op jit(solution)/shard_map/all_gather | solution.py:157
  17.4 0.0 copy-start
  17.4 9.8 %shard_map.84 = (bf16[128,64,128]{2,1,0:T(8,128)(2,1)}, bf16[64,64,128]{2,1,0:T(8,128)(2,1)}, bf16[64,64,128]{2,1,0:T(8,128)(2,1)}) custom-call(s32[1,256]{1,0:T(1,128)} %ids_ref.3, bf16[64,4096]{1,0:T(8,128)(2,1)} %gate_ref.3, bf16[64,4096]{1,0:T(8,128)(2,1)} %up_ref.3, bf16[64,4096]{1,0:T(8,128)(2,1)} %all_gather.3.cot_ref), custom_call_target="tpu_custom_call" | custom-call | flops 1000000000 | bytes 8388608 | tf_op jit(solution)/shard_map/pallas_call | solution.py:159
  27.2 0.0 reduce-scatter.2.cloned.1.call-update
  27.2 0.0 copy-done
  27.2 5.5 %reshape_squeeze.3 = bf16[8,2,16,64,64]{4,3,2,1,0:T(8,128)(2,1)} reshape(bf16[1,256,4096]{2,1,0:T(8,128)(2,1)S(1)} %copy-done) | data formatting | bytes 4194304 | tf_op jit(solution)/shard_map/reshape;squeeze | solution.py:167
  32.8 12.6 %copy.12 = bf16[8,2,16,64,64]{4,1,3,2,0:T(2,128)(2,1)} copy(bf16[8,2,16,64,64]{4,3,2,1,0:T(8,128)(2,1)} %reshape_squeeze.3) | data formatting | bytes 4194304 | tf_op jit(solution)/shard_map/reshape;squeeze | solution.py:167
  45.4 7.8 %reshape.24.w_ref = bf16[128,64,128]{2,1,0:T(8,128)(2,1)} reshape(bf16[8,16,64,2,64]{4,3,2,1,0:T(2,128)(2,1)} %bitcast.7) | data formatting | bytes 4194304 | tf_op jit(solution)/shard_map/reshape | solution.py:168
  53.2 13.3 %shard_map.85 = (bf16[64,4096]{1,0:T(8,128)(2,1)}, bf16[64,4096]{1,0:T(8,128)(2,1)}, bf16[64,4096]{1,0:T(8,128)(2,1)}) custom-call(s32[1,256]{1,0:T(1,128)} %ids_ref.3, bf16[64,4096]{1,0:T(8,128)(2,1)} %gate_ref.3, bf16[64,4096]{1,0:T(8,128)(2,1)} %up_ref.3, bf16[64,64,128]{2,1,0:T(8,128)(2,1)} %get-tuple-element.10.ht_ref, ...), custom_call_target="tpu_custom_call" | custom-call | flops 1000000000 | bytes 16777216 | tf_op jit(solution)/shard_map/pallas_call | solution.py:170
  66.6 12.3 %all_to_all.5 = bf16[4,16,4096]{2,1,0:T(8,128)(2,1)S(1)} all-to-all(bf16[4,16,4096]{2,1,0:T(8,128)(2,1)} %bitcast.9), channel_id=1, replica_groups=mesh['dp'=8,'tensor'=4] {'tensor'}, dimensions={0} | all-to-all | bytes 1048576 | tf_op jit(solution)/shard_map/all_to_all | solution.py:178
  78.8 0.7 reduce_sum.12
  79.6 16.4 %reduce-scatter.2.cloned.1.call-done = bf16[16,64,128]{2,1,0:T(8,128)(2,1)} async-done(((bf16[128,64,128]{2,1,0:T(8,128)(2,1)}), bf16[16,64,128]{2,1,0:T(8,128)(2,1)}) %reduce-scatter.2.cloned.1.call-update) | async-done | bytes 262160 | tf_op jit(solution)/shard_map/reduce_scatter | solution.py:166
  95.9 1.5 %reshape.33 = f32[16,64,2,64]{3,2,1,0:T(2,128)S(1)} reshape(bf16[16,64,128]{2,1,0:T(8,128)(2,1)} %reduce-scatter.2.cloned.1.call-done) | data formatting | bytes 786432 | tf_op jit(solution)/shard_map/reshape | solution.py:181
  97.5 0.1 copy.10
  97.6 1.2 %reshape.30 = f32[1,32,4096]{2,1,0:T(8,128)} reshape(f32[2,16,64,64]{3,2,1,0:T(8,128)S(1)} %copy.10) | data formatting | bytes 1048576 | tf_op jit(solution)/shard_map/reshape | solution.py:181
Async XLA Ops:
  7.2 88.8 %reduce-scatter.2.cloned.1.call-start = ((), (), s32[]{:S(2)}) async-start(), calls=%async_computation.2 | async-start | bytes 2359296 | tf_op jit(solution)/shard_map/reduce_scatter | solution.py:166
  17.4 9.8 %copy-start = (bf16[1,256,4096]{2,1,0:T(8,128)(2,1)S(1)}, bf16[1,256,4096]{2,1,0:T(8,128)(2,1)}, u32[]{:S(2)}) copy-start(bf16[1,256,4096]{2,1,0:T(8,128)(2,1)} %param.8) | copy-start | bytes 6291460
Sparse Core Ops, SparseCore 0:
  27.3 68.5 reduce-scatter.1
